TPU v7x, 256 devices: a whole 4x4x8 slice. The times are simulated.
256 devices in a mesh: blk: 64 (over z, x, y_hi), grp: 4 (over y_lo, core).
Axes of the slice: x: 4, y: 4 (y_hi: 2, y_lo: 2; y = y_hi * 2 + y_lo), z: 8, core: 2. Of those that a mesh axis runs over, the one named last changes fastest.
Arguments:
- query_rows: bfloat16 [32768, 128], P(('blk', 'grp')), may hold values from -36 to 36
- key_rows: bfloat16 [32768, 128], P(('blk', 'grp')), may hold values from -6 to 6
- value_rows: bfloat16 [32768, 128], P(('blk', 'grp')), may hold values from -6 to 6
- query_tangent: bfloat16 [32768, 128], P(('blk', 'grp')), may hold values from -6 to 6
- key_tangent: bfloat16 [32768, 128], P(('blk', 'grp')), may hold values from -6 to 6
- value_tangent: bfloat16 [32768, 128], P(('blk', 'grp')), may hold values from -6 to 6
Outputs:
- attended: float32 [32768, 128], P(('blk', 'grp'))
- tangent_out: float32 [32768, 128], P(('blk', 'grp'))
All inputs are finite; a program needn't handle non-finite values.
Results may differ from a plain program's by a relative error of at most 0.02.
Values may be sent and summed in bfloat16 or wider, within the bound.
A program may use at most 128 MiB of HBM per device.

v0:
```python
import jax
import jax.numpy as jnp
from jax import lax
from jax.sharding import PartitionSpec as P


def sent_together(arrays, axis, dim, along):
    ends, at = ([], 0)
    for a in arrays[:-1]:
        at += a.shape[along]
        ends.append(at)
    both = jnp.concatenate(arrays, axis=along)
    return tuple(jnp.split(lax.all_gather(both, axis, axis=dim, tiled=True), ends, axis=along))


def in_one_piece(arrays, axis, split_dim, concat_dim, along):
    both = jnp.concatenate(arrays, axis=along)
    filled, at, gathered = (
        lax.all_to_all(both, axis, split_axis=split_dim, concat_axis=concat_dim, tiled=True),
        0,
        [],
    )
    for a in arrays:
        gathered.append(lax.slice_in_dim(filled, at, at + a.shape[along], axis=along))
        at += a.shape[along]
    return tuple(gathered)


def fresh_state(count, head_size):
    return (
        jnp.full((count, 1), -jnp.inf, jnp.float32),
        jnp.zeros((count, 1), jnp.float32),
        jnp.zeros((count, 1), jnp.float32),
        jnp.zeros((count, head_size), jnp.float32),
        jnp.zeros((count, head_size), jnp.float32),
    )


def panel_update(running, pieces, query_part, tangent_part, score_scale):
    row_max, row_total, slope_total, primal_sum, tangent_sum = running
    key_part, value_part, key_slope, value_slope = pieces
    scores = (
        jnp.einsum("qd,kd->qk", query_part, key_part, preferred_element_type=jnp.float32)
        * score_scale
    )
    slopes = (
        jnp.einsum("qd,kd->qk", tangent_part, key_part, preferred_element_type=jnp.float32)
        + jnp.einsum("qd,kd->qk", query_part, key_slope, preferred_element_type=jnp.float32)
    ) * score_scale
    new_max = jnp.max(scores, axis=1, keepdims=True)
    rescale = jnp.exp(row_max - new_max)
    probs = jnp.exp(scores - new_max)
    weighted = probs * slopes
    probs_low = probs.astype(jnp.bfloat16)
    weighted_low = weighted.astype(jnp.bfloat16)
    return (
        new_max,
        row_total * rescale + jnp.sum(probs, axis=1, keepdims=True),
        slope_total * rescale + jnp.sum(weighted, axis=1, keepdims=True),
        primal_sum * rescale + jnp.dot(probs_low, value_part, preferred_element_type=jnp.float32),
        tangent_sum * rescale
        + jnp.dot(probs_low, value_slope, preferred_element_type=jnp.float32)
        + jnp.dot(weighted_low, value_part, preferred_element_type=jnp.float32),
    )


def finish(state):
    row_max, row_total, slope_total, primal_sum, tangent_sum = state
    attended = primal_sum / row_total
    return (attended, tangent_sum / row_total - slope_total / row_total * attended)


def on_device(query_rows, key_rows, value_rows, query_tangent, key_tangent, value_tangent):
    own_rows, head_size = query_rows.shape
    score_scale = head_size ** (-0.5)
    group_size = lax.axis_size("grp")
    query_panel, tangent_panel = sent_together((query_rows, query_tangent), "grp", 0, 1)
    state = panel_update(
        fresh_state(own_rows * group_size, head_size),
        sent_together((key_rows, value_rows, key_tangent, value_tangent), "blk", 0, 1),
        query_panel,
        tangent_panel,
        score_scale,
    )
    row_max, row_total, slope_total, primal_sum, tangent_sum = state
    maxima, totals, slope_parts, primal_parts, tangent_parts = in_one_piece(
        (
            row_max.reshape(group_size, own_rows, 1),
            row_total.reshape(group_size, own_rows, 1),
            slope_total.reshape(group_size, own_rows, 1),
            primal_sum.reshape(group_size, own_rows, head_size),
            tangent_sum.reshape(group_size, own_rows, head_size),
        ),
        "grp",
        0,
        0,
        2,
    )
    overall = jnp.max(maxima, axis=0)
    factor = jnp.exp(maxima - overall)
    merged = (
        overall,
        jnp.sum(factor * totals, axis=0),
        jnp.sum(factor * slope_parts, axis=0),
        jnp.sum(factor * primal_parts, axis=0),
        jnp.sum(factor * tangent_parts, axis=0),
    )
    return finish(merged)


def solution(mesh):
    placed = (
        P(("blk", "grp"), None),
        P(("blk", "grp"), None),
        P(("blk", "grp"), None),
        P(("blk", "grp"), None),
        P(("blk", "grp"), None),
        P(("blk", "grp"), None),
    )
    return jax.shard_map(
        on_device,
        mesh=mesh,
        in_specs=placed,
        out_specs=(P(("blk", "grp"), None), P(("blk", "grp"), None)),
        check_vma=False,
    )
```

profile of v0, /device:TPU:1, one launch (start us, length us, event | category | flops | bytes accessed | tf_op | source)
XLA Modules:
  0.0 251.6 jit_solution(7459588162368085257)
XLA Ops:
  7.2 0.0 all-gather.2.cloned.1.call-start
  7.2 1.5 pad_maximum_fusion
  8.7 0.0 all-gather.2.cloned.1.call-update
  8.7 0.8 pad_maximum_fusion.1
  9.5 8.9 %all_gather.6 = bf16[512,256]{1,0:T(8,128)(2,1)S(1)} all-gather(bf16[128,256]{1,0:T(8,128)(2,1)S(1)} %pad_maximum_fusion.1), channel_id=1, replica_groups=mesh['blk'=64,'grp'=4] {'grp'}, dimensions={0}, use_global_device_ids=true | all-gather | bytes 327680 | tf_op jit(solution)/shard_map/all_gather | solution.py:13
  18.3 141.9 %all-gather.2.cloned.1.call-done = bf16[8192,512]{1,0:T(8,128)(2,1)} async-done(((bf16[128,512]{1,0:T(8,128)(2,1)}), bf16[8192,512]{1,0:T(8,128)(2,1)}) %all-gather.2.cloned.1.call-update) | async-done | bytes 8388624 | tf_op jit(solution)/shard_map/all_gather | solution.py:13
  160.2 9.6 %multiply_reduce_fusion = (f32[512]{0:T(512)S(1)}, f32[512,8192]{1,0:T(8,128)}) fusion(bf16[8192,512]{1,0:T(8,128)(2,1)} %all-gather.2.cloned.1.call-done, bf16[512,256]{1,0:T(8,128)(2,1)S(1)} %all_gather.6), kind=kOutput, calls=%fused_computation.2 | convolution fusion | flops 1082129920 | bytes 19007488 | tf_op jit(solution)/shard_map/qd,kd->qk/dot_general | solution.py:43
  169.9 8.6 %fusion.1 = f32[512]{0:T(512)S(1)} fusion(f32[512,8192]{1,0:T(8,128)} %get-tuple-element.14, f32[512]{0:T(512)S(1)} %get-tuple-element.13), kind=kLoop, calls=%fused_computation.4 | loop fusion | flops 12582400 | bytes 16781312 | tf_op jit(solution)/shard_map/reduce_sum | solution.py:58
  178.5 9.7 %fusion.10 = f32[512,8192]{1,0:T(8,128)} fusion(bf16[8192,512]{1,0:T(8,128)(2,1)} %all-gather.2.cloned.1.call-done, bf16[512,256]{1,0:T(8,128)(2,1)S(1)} %all_gather.6), kind=kOutput, calls=%fused_computation.13 | convolution fusion | flops 1073741824 | bytes 19005440 | tf_op jit(solution)/shard_map/qd,kd->qk/dot_general | solution.py:47
  188.2 17.5 %fusion.34 = (f32[512]{0:T(512)S(1)}, bf16[512,8192]{1,0:T(8,128)(2,1)}) fusion(f32[512,8192]{1,0:T(8,128)} %fusion.10, bf16[8192,512]{1,0:T(8,128)(2,1)} %all-gather.2.cloned.1.call-done, bf16[512,256]{1,0:T(8,128)(2,1)S(1)} %all_gather.6, f32[512]{0:T(512)S(1)} %get-tuple-element.13, f32[512,8192]{1,0:T(8,128)} %get-tuple-element.14), kind=kOutput, calls=%fused_computation.43 | convolution fusion | flops 1103101440 | bytes 44175360 | tf_op jit(solution)/shard_map/qd,kd->qk/dot_general | solution.py:48
  205.6 6.3 %fusion.2 = f32[512,128]{1,0:T(8,128)S(1)} fusion(bf16[512,8192]{1,0:T(8,128)(2,1)} %get-tuple-element.16, bf16[8192,512]{1,0:T(8,128)(2,1)} %all-gather.2.cloned.1.call-done), kind=kOutput, calls=%fused_computation.5 | convolution fusion | flops 1073741824 | bytes 10747904 | tf_op jit(solution)/shard_map/dot_general | solution.py:63
  211.9 8.2 %fusion.20 = f32[512,128]{1,0:T(8,128)S(1)} fusion(f32[512,128]{1,0:T(8,128)S(1)} %fusion.2, bf16[8192,512]{1,0:T(8,128)(2,1)} %all-gather.2.cloned.1.call-done, f32[512]{0:T(512)S(1)} %exponential_multiply_fusion, f32[512,8192]{1,0:T(8,128)} %get-tuple-element.14, f32[512]{0:T(512)S(1)} %get-tuple-element.13), kind=kOutput, calls=%fused_computation.19 | convolution fusion | flops 1086455808 | bytes 19402752 | tf_op jit(solution)/shard_map/dot_general | solution.py:62
  220.1 0.1 copy.14
  220.3 8.2 %fusion.14 = f32[512,128]{1,0:T(8,128)S(1)} fusion(bf16[8192,512]{1,0:T(8,128)(2,1)} %all-gather.2.cloned.1.call-done, f32[512]{0:T(512)S(1)} %exponential_multiply_fusion, f32[512,8192]{1,0:T(8,128)} %get-tuple-element.14, f32[512]{0:T(512)S(1)} %get-tuple-element.13), kind=kOutput, calls=%fused_computation.17 | convolution fusion | flops 1086390272 | bytes 19140608 | tf_op jit(solution)/shard_map/dot_general | solution.py:60
  228.5 0.1 copy.13
  228.6 0.6 concatenate.11
  229.2 14.0 %all_to_all.5 = f32[4,128,259]{1,2,0:T(8,128)S(1)} all-to-all(f32[4,128,259]{1,2,0:T(8,128)S(1)} %concatenate.11), channel_id=1, replica_groups=mesh['blk'=64,'grp'=4] {'grp'}, dimensions={0} | all-to-all | bytes 1060864 | tf_op jit(solution)/shard_map/all_to_all | solution.py:19
  243.2 0.1 fusion.23
  243.3 0.7 copy.18
  244.0 0.7 copy.17
  (6 shorter events, 0.1 us)
Async XLA Ops:
  7.2 153.1 %all-gather.2.cloned.1.call-start = ((), (), s32[]{:S(2)}) async-start(), calls=%async_computation.1 | async-start | bytes 8519680 | tf_op jit(solution)/shard_map/all_gather | solution.py:13
Sparse Core Ops, SparseCore 0:
  11.6 148.5 all-gather.1
where the time goes:
time: 252 us
  waiting for transfers between devices  142 us (56%)
  matrix products  59.4 us (24%)
  blocking collectives  22.8 us (9%)
  between operations  14.1 us (6%)
  other arithmetic  11 us (4%)
    all_gather x1, waiting for transfers between devices, sent_together(): lax.all_gather(both, axis, axis=dim, tiled=True)  142 us
    dot_general x1, matrix products, panel_update(): jnp.einsum('qd,kd->qk', query_part, key_slope, preferred_element_type=jnp...  17.5 us
    all_to_all x1, blocking collectives, in_one_piece(): lax.all_to_all(both, axis, split_axis=split_dim, concat_axis=concat_dim,...  14 us
    dot_general x1, matrix products, panel_update(): jnp.einsum('qd,kd->qk', tangent_part, key_part, preferred_element_type=jn...  9.65 us
    dot_general x1, matrix products, panel_update(): jnp.einsum('qd,kd->qk', query_part, key_part, preferred_element_type=jnp....  9.64 us
    all_gather x1, blocking collectives, sent_together(): lax.all_gather(both, axis, axis=dim, tiled=True)  8.86 us
    reduce_sum x1, other arithmetic, panel_update(): jnp.sum(probs, axis=1, keepdims=True)  8.62 us
    dot_general x1, matrix products, panel_update(): jnp.dot(probs_low, value_slope, preferred_element_type=jnp.float32)  8.18 us
  transfers between devices with their start and end apart: 1, of which 1 were waited for; matrix products, arithmetic and copies ran while one was open for 0% of the time, Pallas kernels for 0%

commit v1 on v0

v1 whole, which is shorter than its diff:
```python
import jax
import jax.numpy as jnp
from jax import lax
from jax.experimental import pallas as pl
from jax.experimental.pallas import tpu as pltpu
from jax.sharding import PartitionSpec as P

HD = 128
TOK = 128
F32, BF16 = jnp.float32, jnp.bfloat16
SCALE = HD ** -0.5
LOG2E = 1.4426950408889634
MESH = pl.DeviceIdType.MESH
NT = (((1,), (1,)), ((), ()))

REL = [(0, 0), (1, 0), (3, 0), (0, 1), (0, 3), (2, 0), (0, 2), (1, 1),
       (1, 3), (3, 1), (3, 3), (2, 1), (2, 3), (1, 2), (3, 2), (2, 2)]
BACK = [REL.index(((4 - a) % 4, (4 - b) % 4)) for a, b in REL]
NQ = 16 * TOK
NK = 16 * TOK
TQ, TK = 1024, 512


def lane_sum(v):
    out = v[:, :128]
    for j in range(1, v.shape[1] // 128):
        out = out + v[:, j * 128:(j + 1) * 128]
    return out


def kernel(q_ref, k_ref, v_ref, qt_ref, kt_ref, vt_ref, att_ref, tan_ref,
           kb, qb, acc, mb, lb, wb, osend, orecv, ssend, srecv, mix,
           q_s, q_r, ring_s, ring_r, part_s, part_r, o_s, o_r, st_s, st_r):
    blk, grp = lax.axis_index("blk"), lax.axis_index("grp")
    z, x = blk // 8, lax.rem(blk // 2, 4)
    y, core = lax.rem(blk, 2) * 2 + grp // 2, lax.rem(grp, 2)

    def dev(dz=0, dx=0, dy=0, dc=0):
        zz, xx, yy = lax.rem(z + dz, 8), lax.rem(x + dx, 4), lax.rem(y + dy, 4)
        return ((zz * 4 + xx) * 2 + yy // 2, lax.rem(yy, 2) * 2 + lax.rem(core + dc, 2))

    right, left, partner = dev(dz=1), dev(dz=7), dev(dc=1)
    peers = [dev(dx=a, dy=b) for a, b in REL]

    kb[0:TOK, 0:128] = kt_ref[...]
    kb[0:TOK, 128:256] = k_ref[...]
    kb[0:TOK, 256:384] = v_ref[...]
    kb[0:TOK, 384:512] = vt_ref[...]
    qb[0:TOK, 0:128] = q_ref[...]
    qb[0:TOK, 128:256] = qt_ref[...]

    barrier = pltpu.get_barrier_semaphore()
    for d in [right, left, partner] + peers[1:]:
        pl.semaphore_signal(barrier, inc=1, device_id=d, device_id_type=MESH)
    pl.semaphore_wait(barrier, 18)

    def copy(src, dst, ss, rs, to):
        return pltpu.make_async_remote_copy(src_ref=src, dst_ref=dst, send_sem=ss, recv_sem=rs,
                                            device_id=to, device_id_type=MESH)

    def own_rows(d):
        return kb.at[pl.ds(d * 256, TOK), :]

    def other_rows(d):
        return kb.at[pl.ds(d * 256 + TOK, TOK), :]

    def ring(d):
        if d < 7:
            src = 0 if d < 3 else d - 2
            return copy(own_rows(src), own_rows(d), ring_s.at[d], ring_r.at[d], right if d % 2 else left)
        src, off, to = (5, 0, right) if d == 7 else (6, 64, left)
        return copy(kb.at[pl.ds(src * 256 + off, 64), :], kb.at[pl.ds(7 * 256 + off, 64), :],
                    ring_s.at[d], ring_r.at[d], to)

    def across(d):
        return copy(own_rows(d), other_rows(d), part_s.at[d], part_r.at[d], partner)

    def query(s):
        b = BACK[s]
        return copy(qb.at[pl.ds(0, TOK), :], qb.at[pl.ds(b * TOK, TOK), :], q_s.at[b], q_r.at[b], peers[s])

    def result(s):
        b = BACK[s]
        return (copy(osend.at[s], orecv.at[b], o_s.at[b], o_r.at[b], peers[s]),
                copy(ssend.at[s], srecv.at[b], st_s.at[b], st_r.at[b], peers[s]))

    ring(1).start()
    ring(2).start()
    across(0).start()
    for s in range(1, 16):
        query(s).start()

    mb[...] = jnp.full_like(mb, -1e30)
    lb[...] = jnp.zeros_like(lb)
    wb[...] = jnp.zeros_like(wb)
    acc[...] = jnp.zeros_like(acc)

    def arrive(d):
        ring(d).wait_recv()
        if d < 7:
            ring(d + 2).start()
            across(d).start()

    def events(b):
        if b == 0:
            arrive(1)
            arrive(2)
            across(0).wait_recv()
            across(1).wait_recv()
            for s in range(1, 8):
                query(BACK[s]).wait_recv()
        elif b == 1:
            for s in range(8, 16):
                query(BACK[s]).wait_recv()
        elif b == 2:
            arrive(3)
            arrive(4)
            across(2).wait_recv()
            across(3).wait_recv()
        elif b == 4:
            arrive(5)
            arrive(6)
            across(4).wait_recv()
            across(5).wait_recv()
        elif b == 6:
            arrive(7)
            arrive(8)
            across(7).start()
            across(6).wait_recv()
            across(7).wait_recv()

    def finish(pn):
        rows = slice(pn * TQ, (pn + 1) * TQ)
        total = jnp.sum(lb[rows, :], axis=1, keepdims=True)
        inv = 1.0 / total
        slope = jnp.sum(wb[rows, :], axis=1, keepdims=True) * inv * SCALE
        att = acc[rows, :128] * inv
        tan = (acc[rows, 128:256] + SCALE * acc[rows, 256:384]) * inv - slope * att
        lane = lax.broadcasted_iota(jnp.int32, (TQ, 128), 1)
        stat = jnp.where(lane == 0, mb[rows, :], jnp.where(lane == 1, total, slope))
        for i in range(TQ // TOK):
            s = pn * (TQ // TOK) + i
            part = slice(i * TOK, (i + 1) * TOK)
            o_to, s_to = (orecv, srecv) if s == 0 else (osend, ssend)
            o_to[s, :, :128] = att[part].astype(BF16)
            o_to[s, :, 128:] = tan[part].astype(BF16)
            s_to[s] = stat[part].T[:8, :]
            if s > 0:
                for c in result(s):
                    c.start()

    def step(b, carry):
        for i in (0, 1, 2, 4, 6):
            @pl.when(b == i)
            def _():
                events(i)

        kp = b // 2
        pn = jnp.where(kp == 3, 1 - lax.rem(b, 2), lax.rem(b, 2))
        rows = pl.ds(pl.multiple_of(pn * TQ, TQ), TQ)
        keys = pl.ds(pl.multiple_of(kp * TK, TK), TK)
        s = lax.dot_general(qb[rows, :128], kb[keys, 128:256], NT, preferred_element_type=F32)
        t = lax.dot_general(qb[rows, :], kb[keys, :256], NT, preferred_element_type=F32)
        m = mb[rows, :]
        new = jnp.maximum(m, jnp.max(s, axis=1, keepdims=True) * (SCALE * LOG2E))
        al = jnp.exp2(m - new)
        p = jnp.exp2(s * (SCALE * LOG2E) - new[:, :1])
        w = p * t
        mb[rows, :] = new
        lb[rows, :] = lb[rows, :] * al + lane_sum(p)
        wb[rows, :] = wb[rows, :] * al + lane_sum(w)
        pv = jnp.dot(p.astype(BF16), kb[keys, 256:512], preferred_element_type=F32)
        wv = jnp.dot(w.astype(BF16), kb[keys, 256:384], preferred_element_type=F32)
        acc[rows, :128] = acc[rows, :128] * al + pv[:, :128]
        acc[rows, 128:256] = acc[rows, 128:256] * al + pv[:, 128:]
        acc[rows, 256:384] = acc[rows, 256:384] * al + wv

        @pl.when(b == 6)
        def _():
            finish(1)

        @pl.when(b == 7)
        def _():
            finish(0)
        return carry

    lax.fori_loop(0, 8, step, 0)

    for s in range(1, 16):
        for c in result(BACK[s]):
            c.wait_recv()
    st = srecv[...]
    m, l, sl = st[:, 0, :], st[:, 1, :], st[:, 2, :]
    wgt = jnp.exp2(m - jnp.max(m, axis=0, keepdims=True)) * l
    wgt = wgt / jnp.sum(wgt, axis=0, keepdims=True)
    mean = jnp.sum(wgt * sl, axis=0, keepdims=True)
    mix[...] = jnp.zeros_like(mix)
    mix[0:16, :] = wgt
    mix[16:32, :] = wgt * (sl - mean)
    col = mix[...].T
    att = jnp.zeros((TOK, HD), F32)
    tan = jnp.zeros((TOK, HD), F32)
    for s in range(16):
        a = orecv[s, :, :128].astype(F32)
        t = orecv[s, :, 128:].astype(F32)
        att = att + col[:, s:s + 1] * a
        tan = tan + col[:, s:s + 1] * t + col[:, 16 + s:17 + s] * a
    att_ref[...] = att
    tan_ref[...] = tan

    for d in range(1, 9):
        ring(d).wait_send()
    for d in range(8):
        across(d).wait_send()
    for s in range(1, 16):
        query(s).wait_send()
        for c in result(s):
            c.wait_send()


def on_device(query_rows, key_rows, value_rows, query_tangent, key_tangent, value_tangent):
    dma = pltpu.SemaphoreType.DMA
    return pl.pallas_call(
        kernel,
        out_shape=(jax.ShapeDtypeStruct((TOK, HD), F32),) * 2,
        in_specs=[pl.BlockSpec(memory_space=pltpu.VMEM)] * 6,
        out_specs=(pl.BlockSpec(memory_space=pltpu.VMEM),) * 2,
        scratch_shapes=[
            pltpu.VMEM((NK, 512), BF16),
            pltpu.VMEM((NQ, 256), BF16),
            pltpu.VMEM((NQ, 384), F32),
            pltpu.VMEM((NQ, 128), F32),
            pltpu.VMEM((NQ, 128), F32),
            pltpu.VMEM((NQ, 128), F32),
            pltpu.VMEM((16, TOK, 256), BF16),
            pltpu.VMEM((16, TOK, 256), BF16),
            pltpu.VMEM((16, 8, TOK), F32),
            pltpu.VMEM((16, 8, TOK), F32),
            pltpu.VMEM((TOK, TOK), F32),
            dma((16,)), dma((16,)), dma((9,)), dma((9,)), dma((8,)), dma((8,)),
            dma((16,)), dma((16,)), dma((16,)), dma((16,)),
        ],
        compiler_params=pltpu.CompilerParams(
            collective_id=0, has_side_effects=True, vmem_limit_bytes=56 << 20),
    )(query_rows, key_rows, value_rows, query_tangent, key_tangent, value_tangent)


def solution(mesh):
    placed = P(("blk", "grp"), None)
    return jax.shard_map(
        on_device,
        mesh=mesh,
        in_specs=(placed,) * 6,
        out_specs=(placed, placed),
        check_vma=False,
    )
```

time: 252 us -> 61.6 us (0.24)
  waiting for transfers between devices: 142 us -> 0 us
  matrix products: 59.4 us -> 0 us
  Pallas kernels: 0 us -> 58.6 us
  blocking collectives: 22.8 us -> 0 us
  between operations: 14.1 us -> 0.65 us
  other arithmetic: 11 us -> 0 us
    all_gather x1 -> x0, waiting for transfers between devices: 142 us -> none  [sent_together(): lax.all_gather(both, axis, axis=dim, tiled=True)]
    dot_general x6 -> x0, matrix products: 59.4 us -> none  [the longest x1 17.5 us: panel_update(): jnp.einsum('qd,kd->qk', query_part, key_slope, preferred_element_type=jnp...]
    pallas_call x0 -> x1, Pallas kernels: none -> 58.6 us  [on_device(): pl.pallas_call(kernel, out_shape=(jax.ShapeDtypeStruct((TOK, HD), F32),)...]
    all_to_all x1 -> x0, blocking collectives: 14 us -> none  [in_one_piece(): lax.all_to_all(both, axis, split_axis=split_dim, concat_axis=concat_dim,...]
    all_gather x1 -> x0, blocking collectives: 8.86 us -> none  [sent_together(): lax.all_gather(both, axis, axis=dim, tiled=True)]
    reduce_sum x3 -> x0, other arithmetic: 8.72 us -> none  [the longest x1 8.62 us: panel_update(): jnp.sum(probs, axis=1, keepdims=True)]
  transfers between devices with their start and end apart: 1 -> 0, of which waited for: 1 -> 0; matrix products, arithmetic and copies ran while one was open for 0% -> 0% of each run, Pallas kernels for 0% -> 0%
where the time goes in v1:
time: 61.6 us; the launch traced here: 61.4 us
  Pallas kernels  58.6 us (95%)
  local copies, waits for them, and re-layouts  2.14 us (3%)
  between operations  0.65 us (1%)
    pallas_call x1, Pallas kernels, on_device(): pl.pallas_call(kernel, out_shape=(jax.ShapeDtypeStruct((TOK, HD), F32),)...  58.6 us
    unnamed x4, local copies, waits for them, and re-layouts  2.14 us

profile of v1, /device:TPU:1, one launch (start us, length us, event | category | flops | bytes accessed | tf_op | source)
XLA Modules:
  0.0 61.4 jit_solution(6857831722038348251)
XLA Ops:
  0.6 58.6 %shard_map.77 = (f32[128,128]{1,0:T(8,128)}, f32[128,128]{1,0:T(8,128)}) custom-call(bf16[128,128]{1,0:T(8,128)(2,1)} %q_ref.1, bf16[128,128]{1,0:T(8,128)(2,1)} %k_ref.1, bf16[128,128]{1,0:T(8,128)(2,1)} %v_ref.1, bf16[128,128]{1,0:T(8,128)(2,1)} %qt_ref.1, bf16[128,128]{1,0:T(8,128)(2,1)} %kt_ref.1, bf16[128,128]{1,0:T(8,128)(2,1)} %vt_ref.1), custom_call_target="tpu_custom_call" | custom-call | tf_op jit(solution)/shard_map/pallas_call | solution.py:223
  59.2 0.0 copy-start
  59.2 1.5 %copy.10 = f32[128,128]{1,0:T(8,128)} copy(f32[128,128]{1,0:T(8,128)} %get-tuple-element.4) | data formatting | bytes 131072
  60.7 0.0 copy-done
  60.7 0.6 %copy.11 = f32[128,128]{1,0:T(8,128)} copy(f32[128,128]{1,0:T(8,128)S(1)} %copy-done) | data formatting | bytes 131072
Async XLA Ops:
  59.2 1.5 %copy-start = (f32[128,128]{1,0:T(8,128)S(1)}, f32[128,128]{1,0:T(8,128)}, u32[]{:S(2)}) copy-start(f32[128,128]{1,0:T(8,128)} %get-tuple-element.5) | copy-start | bytes 196612

commit v2 on v1

v2 whole, which is shorter than its diff:
```python
import jax
import jax.numpy as jnp
from jax import lax
from jax.experimental import pallas as pl
from jax.experimental.pallas import tpu as pltpu
from jax.sharding import PartitionSpec as P

HD = 128
TOK = 128
HALF = 64
F32, BF16 = jnp.float32, jnp.bfloat16
SCALE = HD ** -0.5
LOG2E = 1.4426950408889634
MESH = pl.DeviceIdType.MESH
NT = (((1,), (1,)), ((), ()))
NQ = 16 * TOK
NK = 16 * TOK

ROWS = ({1: 512, 3: 768, 2: 1536}, {1: 1024, 3: 1280, 2: 1792})
SMALL = [(0, 0), (1, 0), (2, 0), (0, 1), (1, 1), (2, 1)]
LARGE = [(3, 0), (3, 1), (1, 1), (2, 1), (0, 1)]


def lane_sum(v):
    out = v[:, :128]
    for j in range(1, v.shape[1] // 128):
        out = out + v[:, j * 128:(j + 1) * 128]
    return out


def pick(i, table):
    out = table[0]
    for n, v in enumerate(table):
        if n > 0:
            out = jnp.where(i == n, v, out)
    return out


def kernel(q_ref, k_ref, v_ref, qt_ref, kt_ref, vt_ref, att_ref, tan_ref,
           kb, qb, acc, mb, lb, wb, part, stat, part1, stat1, sum1, sstat1, part2, stat2,
           ring_s, ring_r, side_s, side_r, q1_s, q1_r, q2_s, q2_r, o1_s, o1_r, t1_s, t1_r, o2_s, o2_r, t2_s, t2_r):
    blk, grp = lax.axis_index("blk"), lax.axis_index("grp")
    z, x = blk // 8, lax.rem(blk // 2, 4)
    y, core = lax.rem(blk, 2) * 2 + grp // 2, lax.rem(grp, 2)

    def dev(dz=0, dx=0, dy=0, dc=0):
        zz, xx, yy = lax.rem(z + dz, 8), lax.rem(x + dx, 4), lax.rem(y + dy, 4)
        return ((zz * 4 + xx) * 2 + yy // 2, lax.rem(yy, 2) * 2 + lax.rem(core + dc, 2))

    right, left, partner = dev(dz=1), dev(dz=7), dev(dc=1)
    xs, ys = {i: dev(dx=i) for i in (1, 2, 3)}, {i: dev(dy=i) for i in (1, 2, 3)}

    kb[0:TOK, 0:128] = kt_ref[...]
    kb[0:TOK, 128:256] = k_ref[...]
    kb[0:TOK, 256:384] = v_ref[...]
    kb[0:TOK, 384:512] = vt_ref[...]
    for h in (0, 1):
        qb[h * 256:h * 256 + HALF, 0:128] = q_ref[h * HALF:(h + 1) * HALF, :]
        qb[h * 256:h * 256 + HALF, 128:256] = qt_ref[h * HALF:(h + 1) * HALF, :]

    barrier = pltpu.get_barrier_semaphore()
    for d in [right, left, partner] + list(xs.values()) + list(ys.values()):
        pl.semaphore_signal(barrier, inc=1, device_id=d, device_id_type=MESH)
    pl.semaphore_wait(barrier, 9)

    def copy(src, dst, ss, rs, to):
        return pltpu.make_async_remote_copy(src_ref=src, dst_ref=dst, send_sem=ss, recv_sem=rs,
                                            device_id=to, device_id_type=MESH)

    def key_half(d, h, side=0):
        return kb.at[pl.ds(d * 256 + side * TOK + h * HALF, HALF), :]

    def ring(d, h):
        src = 0 if d < 3 else (d - 2 if d < 7 else 5 + h)
        to = (right, left)[h] if d == 7 else (right if d % 2 else left)
        return copy(key_half(src, h), key_half(d, h), ring_s.at[d, h], ring_r.at[d, h], to)

    def across(d, h):
        return copy(key_half(d, h), key_half(d, h, 1), side_s.at[d, h], side_r.at[d, h], partner)

    def query1(h, i):
        b = 4 - i
        return copy(qb.at[pl.ds(h * 256, HALF), :], qb.at[pl.ds(h * 256 + b * HALF, HALF), :],
                    q1_s.at[h, b], q1_r.at[h, b], (xs, ys)[h][i])

    def query2(h, i):
        b = 4 - i
        return copy(qb.at[pl.ds(h * 256, 256), :], qb.at[pl.ds(ROWS[h][b], 256), :],
                    q2_s.at[h, b], q2_r.at[h, b], (ys, xs)[h][i])

    def result1(h, i):
        b, c = 4 - i, ROWS[h][i] // 256
        to = (ys, xs)[h][i]
        return (copy(part.at[c], part1.at[h, b - 1], o1_s.at[h, b], o1_r.at[h, b], to),
                copy(stat.at[c], stat1.at[h, b - 1], t1_s.at[h, b], t1_r.at[h, b], to))

    def result2(h, i):
        b = 4 - i
        to = (xs, ys)[h][i]
        return (copy(sum1.at[h, pl.ds(i * HALF, HALF), :], part2.at[h, b - 1], o2_s.at[h, b], o2_r.at[h, b], to),
                copy(sstat1.at[h], stat2.at[h, b - 1], t2_s.at[h, b], t2_r.at[h, b], to))

    for h in (0, 1):
        ring(1, h).start()
        ring(2, h).start()
        if h == 0:
            for i in (1, 3, 2):
                query1(0, i).start()
                query1(1, i).start()
        across(0, h).start()

    mb[...] = jnp.full_like(mb, -1e30)
    lb[...] = jnp.zeros_like(lb)
    wb[...] = jnp.zeros_like(wb)
    acc[...] = jnp.zeros_like(acc)

    def arrive(d, h):
        ring(d, h).wait_recv()
        if d < 5:
            ring(d + 2, h).start()
        elif d == 5 + h:
            ring(7, h).start()
        across(d, h).start()

    def side(*slots):
        for d in slots:
            across(d, 0).wait_recv()
            across(d, 1).wait_recv()

    def small_events(b):
        if b == 0:
            arrive(1, 0)
            arrive(2, 0)
            for i in (1, 3, 2):
                query1(0, i).wait_recv()
                query1(1, i).wait_recv()
            for i in (1, 3, 2):
                query2(0, i).start()
                query2(1, i).start()
            arrive(1, 1)
            arrive(2, 1)
            side(0, 1)
        elif b == 1:
            arrive(3, 0)
            arrive(4, 0)
            query2(0, 1).wait_recv()
            query2(0, 3).wait_recv()
        elif b == 2:
            arrive(3, 1)
            arrive(4, 1)
            query2(1, 1).wait_recv()
            query2(1, 3).wait_recv()
        elif b == 3:
            arrive(5, 0)
            arrive(6, 0)
            side(2, 3)
        elif b == 4:
            arrive(6, 1)
            arrive(5, 1)

    def large_events(b):
        if b == 0:
            arrive(7, 0)
            arrive(7, 1)
            query2(0, 2).wait_recv()
            query2(1, 2).wait_recv()
        elif b == 1:
            side(4, 5, 6, 7)

    def finish(g):
        rows = slice(g * 512, (g + 1) * 512)
        total = jnp.sum(lb[rows, :], axis=1, keepdims=True)
        inv = 1.0 / total
        slope = jnp.sum(wb[rows, :], axis=1, keepdims=True) * inv * SCALE
        att = acc[rows, :128] * inv
        tan = (acc[rows, 128:256] + SCALE * acc[rows, 256:384]) * inv - slope * att
        lane = lax.broadcasted_iota(jnp.int32, (512, 128), 1)
        col = jnp.where(lane == 0, mb[rows, :], jnp.where(lane == 1, total, slope))
        for i in (0, 1):
            c, here = 2 * g + i, slice(i * 256, (i + 1) * 256)
            part[c, :, :128] = att[here].astype(BF16)
            part[c, :, 128:] = tan[here].astype(BF16)
            for j in (0, 1):
                stat[c, :, j * 128:(j + 1) * 128] = col[i * 256 + j * 128:i * 256 + (j + 1) * 128].T[:8, :]
        for h, i in {1: [(0, 1), (0, 3)], 2: [(1, 1), (1, 3)], 3: [(0, 2), (1, 2)], 0: []}[g]:
            for c in result1(h, i):
                c.start()

    def attend(rows, keys):
        s = lax.dot_general(qb[rows, :128], kb[keys, 128:256], NT, preferred_element_type=F32)
        t = lax.dot_general(qb[rows, :], kb[keys, :256], NT, preferred_element_type=F32)
        m = mb[rows, :]
        new = jnp.maximum(m, jnp.max(s, axis=1, keepdims=True) * (SCALE * LOG2E))
        al = jnp.exp2(m - new)
        p = jnp.exp2(s * (SCALE * LOG2E) - new[:, :1])
        w = p * t
        mb[rows, :] = new
        lb[rows, :] = lb[rows, :] * al + lane_sum(p)
        wb[rows, :] = wb[rows, :] * al + lane_sum(w)
        pv = jnp.dot(p.astype(BF16), kb[keys, 256:512], preferred_element_type=F32)
        wv = jnp.dot(w.astype(BF16), kb[keys, 256:384], preferred_element_type=F32)
        acc[rows, :128] = acc[rows, :128] * al + pv[:, :128]
        acc[rows, 128:256] = acc[rows, 128:256] * al + pv[:, 128:]
        acc[rows, 256:384] = acc[rows, 256:384] * al + wv

    def small(b, carry):
        for i in range(5):
            @pl.when(b == i)
            def _():
                small_events(i)
        g, k = pick(b, [e[0] for e in SMALL]), pick(b, [e[1] for e in SMALL])
        attend(pl.ds(pl.multiple_of(g * 512, 512), 512), pl.ds(pl.multiple_of(k * 512, 512), 512))
        return carry

    def large(b, carry):
        for i in range(2):
            @pl.when(b == i)
            def _():
                large_events(i)
        g, k = pick(b, [e[0] for e in LARGE]), pick(b, [e[1] for e in LARGE])
        attend(pl.ds(pl.multiple_of(g * 512, 512), 512), pl.ds(pl.multiple_of(k * 1024, 1024), 1024))
        for i in range(1, 5):
            @pl.when(b == i)
            def _():
                finish(LARGE[i][0])
        return carry

    lax.fori_loop(0, len(SMALL), small, 0)
    lax.fori_loop(0, len(LARGE), large, 0)

    for h in (0, 1):
        for i in (1, 3, 2):
            for c in result1(h, i):
                c.wait_recv()
        stats = [stat[h]] + [stat1[h, j] for j in range(3)]
        m, l, sl = ([s[r:r + 1, :] for s in stats] for r in range(3))
        top = jnp.maximum(jnp.maximum(m[0], m[1]), jnp.maximum(m[2], m[3]))
        wgt = [jnp.exp2(a - top) * b for a, b in zip(m, l)]
        total = wgt[0] + wgt[1] + wgt[2] + wgt[3]
        inv = 1.0 / total
        wgt = [a * inv for a in wgt]
        mean = wgt[0] * sl[0] + wgt[1] * sl[1] + wgt[2] * sl[2] + wgt[3] * sl[3]
        sstat1[h, 0:1, :] = top
        sstat1[h, 1:2, :] = total
        sstat1[h, 2:3, :] = mean
        sstat1[h, 3:8, :] = jnp.zeros((5, 256), F32)
        both = jnp.concatenate(wgt + [a * (b - mean) for a, b in zip(wgt, sl)], axis=0)
        for j in (0, 1):
            rows = slice(j * 128, (j + 1) * 128)
            col = both[:, rows].T
            att = jnp.zeros((128, HD), F32)
            tan = jnp.zeros((128, HD), F32)
            for n in range(4):
                src = part[h, rows, :] if n == 0 else part1[h, n - 1, rows, :]
                a, t = src[:, :128].astype(F32), src[:, 128:].astype(F32)
                att = att + col[:, n:n + 1] * a
                tan = tan + col[:, n:n + 1] * t + col[:, 4 + n:5 + n] * a
            sum1[h, rows, :128] = att.astype(BF16)
            sum1[h, rows, 128:] = tan.astype(BF16)
        for i in (1, 3, 2):
            for c in result2(h, i):
                c.start()

    for h in (0, 1):
        for i in (1, 3, 2):
            for c in result2(h, i):
                c.wait_recv()
        cols = [sstat1[h, :, 0:128].T[0:HALF, :]]
        srcs = [sum1[h, 0:HALF, :]]
        for b in (1, 2, 3):
            at = (4 - b) * HALF
            lo = at // 128 * 128
            cols.append(stat2[h, b - 1, :, lo:lo + 128].T[at - lo:at - lo + HALF, :])
            srcs.append(part2[h, b - 1])
        m, l, sl = ([c[:, r:r + 1] for c in cols] for r in range(3))
        top = jnp.maximum(jnp.maximum(m[0], m[1]), jnp.maximum(m[2], m[3]))
        wgt = [jnp.exp2(a - top) * b for a, b in zip(m, l)]
        inv = 1.0 / (wgt[0] + wgt[1] + wgt[2] + wgt[3])
        wgt = [a * inv for a in wgt]
        mean = wgt[0] * sl[0] + wgt[1] * sl[1] + wgt[2] * sl[2] + wgt[3] * sl[3]
        att = jnp.zeros((HALF, HD), F32)
        tan = jnp.zeros((HALF, HD), F32)
        for n in range(4):
            a, t = srcs[n][:, :128].astype(F32), srcs[n][:, 128:].astype(F32)
            att = att + wgt[n] * a
            tan = tan + wgt[n] * t + (wgt[n] * (sl[n] - mean)) * a
        att_ref[h * HALF:(h + 1) * HALF, :] = att
        tan_ref[h * HALF:(h + 1) * HALF, :] = tan

    for h in (0, 1):
        for d in range(1, 8):
            ring(d, h).wait_send()
        for d in range(8):
            across(d, h).wait_send()
        for i in (1, 2, 3):
            query1(h, i).wait_send()
            query2(h, i).wait_send()
            for c in result1(h, i) + result2(h, i):
                c.wait_send()


def on_device(query_rows, key_rows, value_rows, query_tangent, key_tangent, value_tangent):
    dma = pltpu.SemaphoreType.DMA
    return pl.pallas_call(
        kernel,
        out_shape=(jax.ShapeDtypeStruct((TOK, HD), F32),) * 2,
        in_specs=[pl.BlockSpec(memory_space=pltpu.VMEM)] * 6,
        out_specs=(pl.BlockSpec(memory_space=pltpu.VMEM),) * 2,
        scratch_shapes=[
            pltpu.VMEM((NK, 512), BF16),
            pltpu.VMEM((NQ, 256), BF16),
            pltpu.VMEM((NQ, 384), F32),
            pltpu.VMEM((NQ, 128), F32),
            pltpu.VMEM((NQ, 128), F32),
            pltpu.VMEM((NQ, 128), F32),
            pltpu.VMEM((8, 256, 256), BF16),
            pltpu.VMEM((8, 8, 256), F32),
            pltpu.VMEM((2, 3, 256, 256), BF16),
            pltpu.VMEM((2, 3, 8, 256), F32),
            pltpu.VMEM((2, 256, 256), BF16),
            pltpu.VMEM((2, 8, 256), F32),
            pltpu.VMEM((2, 3, HALF, 256), BF16),
            pltpu.VMEM((2, 3, 8, 256), F32),
            dma((8, 2)), dma((8, 2)), dma((8, 2)), dma((8, 2)),
            dma((2, 4)), dma((2, 4)), dma((2, 4)), dma((2, 4)),
            dma((2, 4)), dma((2, 4)), dma((2, 4)), dma((2, 4)),
            dma((2, 4)), dma((2, 4)), dma((2, 4)), dma((2, 4)),
        ],
        compiler_params=pltpu.CompilerParams(
            collective_id=0, has_side_effects=True, vmem_limit_bytes=56 << 20),
    )(query_rows, key_rows, value_rows, query_tangent, key_tangent, value_tangent)


def solution(mesh):
    placed = P(("blk", "grp"), None)
    return jax.shard_map(
        on_device,
        mesh=mesh,
        in_specs=(placed,) * 6,
        out_specs=(placed, placed),
        check_vma=False,
    )
```

time: 61.6 us -> 49.2 us (0.80)
  Pallas kernels: 58.6 us -> 46.2 us
    pallas_call x1, Pallas kernels: 58.6 us -> 46.2 us  [on_device(): pl.pallas_call(kernel, out_shape=(jax.ShapeDtypeStruct((TOK, HD), F32),)...]
where the time goes in v2:
time: 49.2 us; the launch traced here: 49 us
  Pallas kernels  46.2 us (94%)
  local copies, waits for them, and re-layouts  2.14 us (4%)
  between operations  0.65 us (1%)
    pallas_call x1, Pallas kernels, on_device(): pl.pallas_call(kernel, out_shape=(jax.ShapeDtypeStruct((TOK, HD), F32),)...  46.2 us
    unnamed x4, local copies, waits for them, and re-layouts  2.14 us

profile of v2, /device:TPU:1, one launch (start us, length us, event | category | flops | bytes accessed | tf_op | source)
XLA Modules:
  0.0 49.0 jit_solution(9250964280547826640)
XLA Ops:
  0.6 46.2 %shard_map.77 = (f32[128,128]{1,0:T(8,128)}, f32[128,128]{1,0:T(8,128)}) custom-call(bf16[128,128]{1,0:T(8,128)(2,1)} %q_ref.1, bf16[128,128]{1,0:T(8,128)(2,1)} %k_ref.1, bf16[128,128]{1,0:T(8,128)(2,1)} %v_ref.1, bf16[128,128]{1,0:T(8,128)(2,1)} %qt_ref.1, bf16[128,128]{1,0:T(8,128)(2,1)} %kt_ref.1, bf16[128,128]{1,0:T(8,128)(2,1)} %vt_ref.1), custom_call_target="tpu_custom_call" | custom-call | tf_op jit(solution)/shard_map/pallas_call | solution.py:304
  46.8 0.0 copy-start
  46.8 1.5 %copy.10 = f32[128,128]{1,0:T(8,128)} copy(f32[128,128]{1,0:T(8,128)} %get-tuple-element.4) | data formatting | bytes 131072
  48.3 0.0 copy-done
  48.3 0.6 %copy.11 = f32[128,128]{1,0:T(8,128)} copy(f32[128,128]{1,0:T(8,128)S(1)} %copy-done) | data formatting | bytes 131072
Async XLA Ops:
  46.8 1.5 %copy-start = (f32[128,128]{1,0:T(8,128)S(1)}, f32[128,128]{1,0:T(8,128)}, u32[]{:S(2)}) copy-start(f32[128,128]{1,0:T(8,128)} %get-tuple-element.5) | copy-start | bytes 196612

commit v3 on v2

v3 whole, which is shorter than its diff:
```python
import jax
import jax.numpy as jnp
from jax import lax
from jax.experimental import pallas as pl
from jax.experimental.pallas import tpu as pltpu
from jax.sharding import PartitionSpec as P

HD = 128
TOK = 128
HALF = 64
F32, BF16 = jnp.float32, jnp.bfloat16
SCALE = HD ** -0.5
LOG2E = 1.4426950408889634
MESH = pl.DeviceIdType.MESH
NT = (((1,), (1,)), ((), ()))
NQ = 16 * TOK
NK = 16 * TOK

UNIT = ({1: (4, 8), 3: (5, 9), 2: (12, 13)}, {1: (6, 10), 3: (7, 11), 2: (14, 15)})
SENT = {UNIT[h][i][p]: (h, i, p) for h in (0, 1) for i in (1, 2, 3) for p in (0, 1)}
SMALL = [(0, 0), (1, 0), (2, 0), (0, 1), (1, 1), (2, 1)]
LARGE = [(3, 0), (3, 1), (1, 1), (2, 1), (0, 1)]


def pick(i, table):
    out = table[0]
    for n, v in enumerate(table):
        if n > 0:
            out = jnp.where(i == n, v, out)
    return out


def kernel(q_ref, k_ref, v_ref, qt_ref, kt_ref, vt_ref, att_ref, tan_ref,
           kb, qb, acc, mb, lb, wb, part, stat, part1, stat1, sum1, sstat1, part2, stat2,
           in_s, ring_s, ring_r, side_s, side_r, q1_s, q1_r, q2_s, q2_r, o1_s, o1_r, t1_s, t1_r, o2_s, o2_r, t2_s, t2_r):
    blk, grp = lax.axis_index("blk"), lax.axis_index("grp")
    z, x = blk // 8, lax.rem(blk // 2, 4)
    y, core = lax.rem(blk, 2) * 2 + grp // 2, lax.rem(grp, 2)

    def dev(dz=0, dx=0, dy=0, dc=0):
        zz, xx, yy = lax.rem(z + dz, 8), lax.rem(x + dx, 4), lax.rem(y + dy, 4)
        return ((zz * 4 + xx) * 2 + yy // 2, lax.rem(yy, 2) * 2 + lax.rem(core + dc, 2))

    right, left, partner = dev(dz=1), dev(dz=7), dev(dc=1)
    xs, ys = {i: dev(dx=i) for i in (1, 2, 3)}, {i: dev(dy=i) for i in (1, 2, 3)}

    barrier = pltpu.get_barrier_semaphore()
    for d in [right, left, partner] + list(xs.values()) + list(ys.values()):
        pl.semaphore_signal(barrier, inc=1, device_id=d, device_id_type=MESH)

    loads = [pltpu.make_async_copy(src, kb.at[pl.ds(0, TOK), pl.ds(n * HD, HD)], in_s.at[n])
             for n, src in enumerate((kt_ref, k_ref, v_ref, vt_ref))]
    for h in (0, 1):
        for n, src in enumerate((q_ref, qt_ref)):
            loads.append(pltpu.make_async_copy(src.at[pl.ds(h * HALF, HALF), :],
                                               qb.at[pl.ds(h * 256, HALF), pl.ds(n * HD, HD)], in_s.at[4 + 2 * h + n]))
    for c in loads:
        c.start()
    for c in loads:
        c.wait()
    pl.semaphore_wait(barrier, 9)

    def copy(src, dst, ss, rs, to):
        return pltpu.make_async_remote_copy(src_ref=src, dst_ref=dst, send_sem=ss, recv_sem=rs,
                                            device_id=to, device_id_type=MESH)

    def key_half(d, h, side=0):
        return kb.at[pl.ds(d * 256 + side * TOK + h * HALF, HALF), :]

    def ring(d, h):
        src = 0 if d < 3 else (d - 2 if d < 7 else 5 + h)
        to = (right, left)[h] if d == 7 else (right if d % 2 else left)
        return copy(key_half(src, h), key_half(d, h), ring_s.at[d, h], ring_r.at[d, h], to)

    def across(d, h):
        return copy(key_half(d, h), key_half(d, h, 1), side_s.at[d, h], side_r.at[d, h], partner)

    def query1(h, i):
        b = 4 - i
        return copy(qb.at[pl.ds(h * 256, HALF), :], qb.at[pl.ds(h * 256 + b * HALF, HALF), :],
                    q1_s.at[h, b], q1_r.at[h, b], (xs, ys)[h][i])

    def query2(h, i, p):
        b = 4 - i
        return copy(qb.at[pl.ds(h * 256 + p * TOK, TOK), :], qb.at[pl.ds(UNIT[h][b][p] * TOK, TOK), :],
                    q2_s.at[h, 2 * b + p], q2_r.at[h, 2 * b + p], (ys, xs)[h][i])

    def result1(h, i, p):
        b, u = 4 - i, UNIT[h][i][p]
        to, n = (ys, xs)[h][i], 2 * b + p
        return (copy(part.at[u], part1.at[h, b - 1, p], o1_s.at[h, n], o1_r.at[h, n], to),
                copy(stat.at[u], stat1.at[h, b - 1, p], t1_s.at[h, n], t1_r.at[h, n], to))

    def result2(h, i):
        b, p = 4 - i, i // 2
        to = (xs, ys)[h][i]
        return (copy(sum1.at[h, p, pl.ds(i % 2 * HALF, HALF), :], part2.at[h, b - 1], o2_s.at[h, b], o2_r.at[h, b], to),
                copy(sstat1.at[h, p], stat2.at[h, b - 1], t2_s.at[h, b], t2_r.at[h, b], to))

    for h in (0, 1):
        ring(1, h).start()
        ring(2, h).start()
        if h == 0:
            for i in (1, 3, 2):
                query1(0, i).start()
                query1(1, i).start()
        across(0, h).start()

    mb[...] = jnp.full_like(mb, -1e30)
    lb[...] = jnp.zeros_like(lb)
    wb[...] = jnp.zeros_like(wb)
    acc[...] = jnp.zeros_like(acc)

    def arrive(d, h):
        ring(d, h).wait_recv()
        if d < 5:
            ring(d + 2, h).start()
        elif d == 5 + h:
            ring(7, h).start()
        across(d, h).start()

    def side(*slots):
        for d in slots:
            across(d, 0).wait_recv()
            across(d, 1).wait_recv()

    def small_events(b):
        if b == 0:
            arrive(1, 0)
            arrive(2, 0)
            for i in (1, 3, 2):
                query1(0, i).wait_recv()
                query1(1, i).wait_recv()
            for p, i in ((0, 1), (0, 3), (1, 1), (1, 3), (0, 2), (1, 2)):
                query2(0, i, p).start()
                query2(1, i, p).start()
            arrive(1, 1)
            arrive(2, 1)
            side(0, 1)
        elif b == 1:
            arrive(3, 0)
            arrive(4, 0)
            near(0)
        elif b == 2:
            arrive(3, 1)
            arrive(4, 1)
            near(1)
        elif b == 3:
            side(2, 3)
        elif b == 4:
            arrive(5, 0)
            arrive(6, 0)
        elif b == 5:
            arrive(6, 1)
            arrive(5, 1)

    def near(p):
        for i in (1, 3):
            query2(0, i, p).wait_recv()
            query2(1, i, p).wait_recv()

    def large_events(b):
        if b == 0:
            for p in (0, 1):
                query2(0, 2, p).wait_recv()
                query2(1, 2, p).wait_recv()
            arrive(7, 0)
            arrive(7, 1)
        elif b == 1:
            side(4, 5, 6, 7)

    def finish(g):
        for u in range(4 * g, 4 * g + 4):
            rows = slice(u * TOK, (u + 1) * TOK)
            total = jnp.sum(lb[rows, :], axis=1, keepdims=True)
            inv = 1.0 / total
            slope = jnp.sum(wb[rows, :], axis=1, keepdims=True) * inv * SCALE
            att = acc[rows, :128] * inv
            tan = (acc[rows, 128:256] + SCALE * acc[rows, 256:384]) * inv - slope * att
            part[u, :, :128] = att.astype(BF16)
            part[u, :, 128:] = tan.astype(BF16)
            lane = lax.broadcasted_iota(jnp.int32, (TOK, 128), 1)
            stat[u] = jnp.where(lane == 0, mb[rows, :], jnp.where(lane == 1, total, slope)).T[:8, :]
            if u >= 4:
                for c in result1(*SENT[u]):
                    c.start()

    def attend(rows, keys, groups):
        s = lax.dot_general(qb[rows, :128], kb[keys, 128:256], NT, preferred_element_type=F32)
        t = lax.dot_general(qb[rows, :], kb[keys, :256], NT, preferred_element_type=F32)
        cut = [slice(j * 128, (j + 1) * 128) for j in range(groups)]
        top = s[:, cut[0]]
        for j in cut[1:]:
            top = jnp.maximum(top, s[:, j])
        top = jnp.broadcast_to(jnp.max(top, axis=1, keepdims=True), top.shape) * (SCALE * LOG2E)
        m = mb[rows, :]
        new = jnp.maximum(m, top)
        al = jnp.exp2(m - new)
        p = [jnp.exp2(s[:, j] * (SCALE * LOG2E) - new) for j in cut]
        w = [a * t[:, j] for a, j in zip(p, cut)]
        mb[rows, :] = new
        lb[rows, :] = lb[rows, :] * al + sum(p[1:], p[0])
        wb[rows, :] = wb[rows, :] * al + sum(w[1:], w[0])
        p = jnp.concatenate([a.astype(BF16) for a in p], axis=1)
        w = jnp.concatenate([a.astype(BF16) for a in w], axis=1)
        pv = jnp.dot(p, kb[keys, 256:512], preferred_element_type=F32)
        wv = jnp.dot(w, kb[keys, 256:384], preferred_element_type=F32)
        acc[rows, :128] = acc[rows, :128] * al + pv[:, :128]
        acc[rows, 128:256] = acc[rows, 128:256] * al + pv[:, 128:]
        acc[rows, 256:384] = acc[rows, 256:384] * al + wv

    def small(b, carry):
        for i in range(6):
            @pl.when(b == i)
            def _():
                small_events(i)
        g, k = pick(b, [e[0] for e in SMALL]), pick(b, [e[1] for e in SMALL])
        attend(pl.ds(pl.multiple_of(g * 512, 512), 512), pl.ds(pl.multiple_of(k * 512, 512), 512), 4)
        return carry

    def large(b, carry):
        for i in range(2):
            @pl.when(b == i)
            def _():
                large_events(i)
        g, k = pick(b, [e[0] for e in LARGE]), pick(b, [e[1] for e in LARGE])
        attend(pl.ds(pl.multiple_of(g * 512, 512), 512), pl.ds(pl.multiple_of(k * 1024, 1024), 1024), 8)
        for i in range(1, 5):
            @pl.when(b == i)
            def _():
                finish(LARGE[i][0])
        return carry

    lax.fori_loop(0, len(SMALL), small, 0)
    lax.fori_loop(0, len(LARGE), large, 0)

    for p, h in ((0, 0), (0, 1), (1, 0), (1, 1)):
        for i in (2, 1, 3):
            for c in result1(h, i, p):
                c.wait_recv()
        stats = [stat[2 * h + p]] + [stat1[h, j, p] for j in range(3)]
        m, l, sl = ([s[r:r + 1, :] for s in stats] for r in range(3))
        top = jnp.maximum(jnp.maximum(m[0], m[1]), jnp.maximum(m[2], m[3]))
        wgt = [jnp.exp2(a - top) * b for a, b in zip(m, l)]
        total = wgt[0] + wgt[1] + wgt[2] + wgt[3]
        inv = 1.0 / total
        wgt = [a * inv for a in wgt]
        mean = wgt[0] * sl[0] + wgt[1] * sl[1] + wgt[2] * sl[2] + wgt[3] * sl[3]
        sstat1[h, p, 0:1, :] = top
        sstat1[h, p, 1:2, :] = total
        sstat1[h, p, 2:3, :] = mean
        sstat1[h, p, 3:8, :] = jnp.zeros((5, TOK), F32)
        col = jnp.concatenate(wgt + [a * (b - mean) for a, b in zip(wgt, sl)], axis=0).T
        att = jnp.zeros((TOK, HD), F32)
        tan = jnp.zeros((TOK, HD), F32)
        for n in range(4):
            src = part[2 * h + p] if n == 0 else part1[h, n - 1, p]
            a, t = src[:, :128].astype(F32), src[:, 128:].astype(F32)
            att = att + col[:, n:n + 1] * a
            tan = tan + col[:, n:n + 1] * t + col[:, 4 + n:5 + n] * a
        sum1[h, p, :, :128] = att.astype(BF16)
        sum1[h, p, :, 128:] = tan.astype(BF16)
        for i in ((1,), (2, 3))[p]:
            for c in result2(h, i):
                c.start()

    for h in (0, 1):
        for i in (1, 3, 2):
            for c in result2(h, i):
                c.wait_recv()
        cols = [sstat1[h, 0].T[0:HALF, :]]
        srcs = [sum1[h, 0, 0:HALF, :]]
        for b in (1, 2, 3):
            at = (4 - b) % 2 * HALF
            cols.append(stat2[h, b - 1].T[at:at + HALF, :])
            srcs.append(part2[h, b - 1])
        m, l, sl = ([c[:, r:r + 1] for c in cols] for r in range(3))
        top = jnp.maximum(jnp.maximum(m[0], m[1]), jnp.maximum(m[2], m[3]))
        wgt = [jnp.exp2(a - top) * b for a, b in zip(m, l)]
        inv = 1.0 / (wgt[0] + wgt[1] + wgt[2] + wgt[3])
        wgt = [a * inv for a in wgt]
        mean = wgt[0] * sl[0] + wgt[1] * sl[1] + wgt[2] * sl[2] + wgt[3] * sl[3]
        att = jnp.zeros((HALF, HD), F32)
        tan = jnp.zeros((HALF, HD), F32)
        for n in range(4):
            a, t = srcs[n][:, :128].astype(F32), srcs[n][:, 128:].astype(F32)
            att = att + wgt[n] * a
            tan = tan + wgt[n] * t + (wgt[n] * (sl[n] - mean)) * a
        att_ref[h * HALF:(h + 1) * HALF, :] = att
        tan_ref[h * HALF:(h + 1) * HALF, :] = tan

    for h in (0, 1):
        for d in range(1, 8):
            ring(d, h).wait_send()
        for d in range(8):
            across(d, h).wait_send()
        for i in (1, 2, 3):
            query1(h, i).wait_send()
            query2(h, i, 0).wait_send()
            query2(h, i, 1).wait_send()
            for c in result1(h, i, 0) + result1(h, i, 1) + result2(h, i):
                c.wait_send()


def on_device(query_rows, key_rows, value_rows, query_tangent, key_tangent, value_tangent):
    dma = pltpu.SemaphoreType.DMA
    return pl.pallas_call(
        kernel,
        out_shape=(jax.ShapeDtypeStruct((TOK, HD), F32),) * 2,
        in_specs=[pl.BlockSpec(memory_space=pl.ANY)] * 6,
        out_specs=(pl.BlockSpec(memory_space=pltpu.VMEM),) * 2,
        scratch_shapes=[
            pltpu.VMEM((NK, 512), BF16),
            pltpu.VMEM((NQ, 256), BF16),
            pltpu.VMEM((NQ, 384), F32),
            pltpu.VMEM((NQ, 128), F32),
            pltpu.VMEM((NQ, 128), F32),
            pltpu.VMEM((NQ, 128), F32),
            pltpu.VMEM((16, TOK, 256), BF16),
            pltpu.VMEM((16, 8, TOK), F32),
            pltpu.VMEM((2, 3, 2, TOK, 256), BF16),
            pltpu.VMEM((2, 3, 2, 8, TOK), F32),
            pltpu.VMEM((2, 2, TOK, 256), BF16),
            pltpu.VMEM((2, 2, 8, TOK), F32),
            pltpu.VMEM((2, 3, HALF, 256), BF16),
            pltpu.VMEM((2, 3, 8, TOK), F32),
            dma((8,)), dma((8, 2)), dma((8, 2)), dma((8, 2)), dma((8, 2)),
            dma((2, 4)), dma((2, 4)), dma((2, 8)), dma((2, 8)),
            dma((2, 8)), dma((2, 8)), dma((2, 8)), dma((2, 8)),
            dma((2, 4)), dma((2, 4)), dma((2, 4)), dma((2, 4)),
        ],
        compiler_params=pltpu.CompilerParams(
            collective_id=0, has_side_effects=True, vmem_limit_bytes=56 << 20),
    )(query_rows, key_rows, value_rows, query_tangent, key_tangent, value_tangent)


def solution(mesh):
    placed = P(("blk", "grp"), None)
    return jax.shard_map(
        on_device,
        mesh=mesh,
        in_specs=(placed,) * 6,
        out_specs=(placed, placed),
        check_vma=False,
    )
```

time: 49.2 us -> 46.8 us (0.951)
  Pallas kernels: 46.2 us -> 43.6 us
    pallas_call x1, Pallas kernels: 46.2 us -> 43.6 us  [on_device(): pl.pallas_call(kernel, out_shape=(jax.ShapeDtypeStruct((TOK, HD), F32),)...]
where the time goes in v3:
time: 46.8 us; the launch traced here: 46.4 us
  Pallas kernels  43.6 us (93%)
  local copies, waits for them, and re-layouts  2.14 us (5%)
  between operations  0.65 us (1%)
    pallas_call x1, Pallas kernels, on_device(): pl.pallas_call(kernel, out_shape=(jax.ShapeDtypeStruct((TOK, HD), F32),)...  43.6 us
    unnamed x4, local copies, waits for them, and re-layouts  2.14 us

profile of v3, /device:TPU:1, one launch (start us, length us, event | category | flops | bytes accessed | tf_op | source)
XLA Modules:
  0.0 46.4 jit_solution(8106191510498885548)
XLA Ops:
  0.6 43.6 %shard_map.77 = (f32[128,128]{1,0:T(8,128)}, f32[128,128]{1,0:T(8,128)}) custom-call(bf16[128,128]{1,0:T(8,128)(2,1)} %q_ref.1, bf16[128,128]{1,0:T(8,128)(2,1)} %k_ref.1, bf16[128,128]{1,0:T(8,128)(2,1)} %v_ref.1, bf16[128,128]{1,0:T(8,128)(2,1)} %qt_ref.1, bf16[128,128]{1,0:T(8,128)(2,1)} %kt_ref.1, bf16[128,128]{1,0:T(8,128)(2,1)} %vt_ref.1), custom_call_target="tpu_custom_call" | custom-call | tf_op jit(solution)/shard_map/pallas_call | solution.py:307
  44.3 0.0 copy-start
  44.3 1.5 %copy.10 = f32[128,128]{1,0:T(8,128)} copy(f32[128,128]{1,0:T(8,128)} %get-tuple-element.4) | data formatting | bytes 131072
  45.8 0.0 copy-done
  45.8 0.6 %copy.11 = f32[128,128]{1,0:T(8,128)} copy(f32[128,128]{1,0:T(8,128)S(1)} %copy-done) | data formatting | bytes 131072
Async XLA Ops:
  44.3 1.5 %copy-start = (f32[128,128]{1,0:T(8,128)S(1)}, f32[128,128]{1,0:T(8,128)}, u32[]{:S(2)}) copy-start(f32[128,128]{1,0:T(8,128)} %get-tuple-element.5) | copy-start | bytes 196612

commit v4 on v3

--- a/solution.py
+++ b/solution.py
@@ -30,7 +30,7 @@
     return out
 
 
-def kernel(q_ref, k_ref, v_ref, qt_ref, kt_ref, vt_ref, att_ref, tan_ref,
+def kernel(q_ref, k_ref, v_ref, qt_ref, kt_ref, vt_ref, out_ref,
            kb, qb, acc, mb, lb, wb, part, stat, part1, stat1, sum1, sstat1, part2, stat2,
            in_s, ring_s, ring_r, side_s, side_r, q1_s, q1_r, q2_s, q2_r, o1_s, o1_r, t1_s, t1_r, o2_s, o2_r, t2_s, t2_r):
     blk, grp = lax.axis_index("blk"), lax.axis_index("grp")
@@ -234,6 +234,16 @@
     lax.fori_loop(0, len(SMALL), small, 0)
     lax.fori_loop(0, len(LARGE), large, 0)
 
+    for h in (0, 1):
+        for d in range(1, 8):
+            ring(d, h).wait_send()
+        for d in range(8):
+            across(d, h).wait_send()
+        for i in (1, 2, 3):
+            query1(h, i).wait_send()
+            query2(h, i, 0).wait_send()
+            query2(h, i, 1).wait_send()
+
     for p, h in ((0, 0), (0, 1), (1, 0), (1, 1)):
         for i in (2, 1, 3):
             for c in result1(h, i, p):
@@ -265,6 +275,11 @@
                 c.start()
 
     for h in (0, 1):
+        for i in (1, 2, 3):
+            for c in result1(h, i, 0) + result1(h, i, 1):
+                c.wait_send()
+
+    for h in (0, 1):
         for i in (1, 3, 2):
             for c in result2(h, i):
                 c.wait_recv()
@@ -286,29 +301,22 @@
             a, t = srcs[n][:, :128].astype(F32), srcs[n][:, 128:].astype(F32)
             att = att + wgt[n] * a
             tan = tan + wgt[n] * t + (wgt[n] * (sl[n] - mean)) * a
-        att_ref[h * HALF:(h + 1) * HALF, :] = att
-        tan_ref[h * HALF:(h + 1) * HALF, :] = tan
-
-    for h in (0, 1):
-        for d in range(1, 8):
-            ring(d, h).wait_send()
-        for d in range(8):
-            across(d, h).wait_send()
+        out_ref[h * HALF:(h + 1) * HALF, :] = att
+        out_ref[TOK + h * HALF:TOK + (h + 1) * HALF, :] = tan
+
+    for h in (0, 1):
         for i in (1, 2, 3):
-            query1(h, i).wait_send()
-            query2(h, i, 0).wait_send()
-            query2(h, i, 1).wait_send()
-            for c in result1(h, i, 0) + result1(h, i, 1) + result2(h, i):
+            for c in result2(h, i):
                 c.wait_send()
 
 
 def on_device(query_rows, key_rows, value_rows, query_tangent, key_tangent, value_tangent):
     dma = pltpu.SemaphoreType.DMA
-    return pl.pallas_call(
+    both = pl.pallas_call(
         kernel,
-        out_shape=(jax.ShapeDtypeStruct((TOK, HD), F32),) * 2,
+        out_shape=jax.ShapeDtypeStruct((2 * TOK, HD), F32),
         in_specs=[pl.BlockSpec(memory_space=pl.ANY)] * 6,
-        out_specs=(pl.BlockSpec(memory_space=pltpu.VMEM),) * 2,
+        out_specs=pl.BlockSpec(memory_space=pltpu.VMEM),
         scratch_shapes=[
             pltpu.VMEM((NK, 512), BF16),
             pltpu.VMEM((NQ, 256), BF16),
@@ -330,8 +338,9 @@
             dma((2, 4)), dma((2, 4)), dma((2, 4)), dma((2, 4)),
         ],
         compiler_params=pltpu.CompilerParams(
-            collective_id=0, has_side_effects=True, vmem_limit_bytes=56 << 20),
-    )(query_rows, key_rows, value_rows, query_tangent, key_tangent, value_tangent)
+            collective_id=0, has_side_effects=True, vmem_limit_bytes=32 << 20),
+    )(*[pltpu.with_memory_space_constraint(a, pltpu.HBM) for a in (query_rows, key_rows, value_rows, query_tangent, key_tangent, value_tangent)])
+    return both[:TOK], both[TOK:]
 
 
 def solution(mesh):

time: 46.8 us -> 44.5 us (0.951)
  local copies, waits for them, and re-layouts: 2.14 us -> 0.66 us
  Pallas kernels: 43.6 us -> 42.9 us
    unnamed x4 -> x0, local copies, waits for them, and re-layouts: 2.14 us -> none
    pallas_call x1, Pallas kernels: 43.6 us -> 42.9 us  [on_device(): pl.pallas_call(kernel, out_shape=jax.ShapeDtypeStruct((2 * TOK, HD), F32)...]
    slice x0 -> x1, local copies, waits for them, and re-layouts: none -> 0.66 us  [on_device(): return (both[:TOK], both[TOK:])]
where the time goes in v4:
time: 44.5 us; the launch traced here: 44.2 us
  Pallas kernels  42.9 us (96%)
  local copies, waits for them, and re-layouts  0.66 us (1%)
  between operations  0.64 us (1%)
    pallas_call x1, Pallas kernels, on_device(): pl.pallas_call(kernel, out_shape=jax.ShapeDtypeStruct((2 * TOK, HD), F32)...  42.9 us

profile of v4, /device:TPU:1, one launch (start us, length us, event | category | flops | bytes accessed | tf_op | source)
XLA Modules:
  0.0 44.2 jit_solution(15055879496617835626)
XLA Ops:
  0.6 42.9 %shard_map.77 = f32[256,128]{1,0:T(8,128)S(1)} custom-call(bf16[128,128]{1,0:T(8,128)(2,1)} %q_ref.1, bf16[128,128]{1,0:T(8,128)(2,1)} %k_ref.1, bf16[128,128]{1,0:T(8,128)(2,1)} %v_ref.1, bf16[128,128]{1,0:T(8,128)(2,1)} %qt_ref.1, bf16[128,128]{1,0:T(8,128)(2,1)} %kt_ref.1, bf16[128,128]{1,0:T(8,128)(2,1)} %vt_ref.1), custom_call_target="tpu_custom_call" | custom-call | tf_op jit(solution)/shard_map/pallas_call | solution.py:315
  43.6 0.7 %fusion = (f32[128,128]{1,0:T(8,128)}, f32[128,128]{1,0:T(8,128)}) fusion(f32[256,128]{1,0:T(8,128)S(1)} %shard_map.77), kind=kLoop, calls=%fused_computation | loop fusion | bytes 262144 | tf_op jit(solution)/shard_map/slice | solution.py:343

commit v5 on v4

--- a/solution.py
+++ b/solution.py
@@ -146,11 +146,10 @@
             arrive(4, 1)
             near(1)
         elif b == 3:
+            arrive(5, 0)
+            arrive(6, 0)
             side(2, 3)
         elif b == 4:
-            arrive(5, 0)
-            arrive(6, 0)
-        elif b == 5:
             arrive(6, 1)
             arrive(5, 1)
 
@@ -185,29 +184,44 @@
                 for c in result1(*SENT[u]):
                     c.start()
 
-    def attend(rows, keys, groups):
-        s = lax.dot_general(qb[rows, :128], kb[keys, 128:256], NT, preferred_element_type=F32)
-        t = lax.dot_general(qb[rows, :], kb[keys, :256], NT, preferred_element_type=F32)
-        cut = [slice(j * 128, (j + 1) * 128) for j in range(groups)]
-        top = s[:, cut[0]]
-        for j in cut[1:]:
-            top = jnp.maximum(top, s[:, j])
-        top = jnp.broadcast_to(jnp.max(top, axis=1, keepdims=True), top.shape) * (SCALE * LOG2E)
-        m = mb[rows, :]
-        new = jnp.maximum(m, top)
-        al = jnp.exp2(m - new)
-        p = [jnp.exp2(s[:, j] * (SCALE * LOG2E) - new) for j in cut]
-        w = [a * t[:, j] for a, j in zip(p, cut)]
-        mb[rows, :] = new
-        lb[rows, :] = lb[rows, :] * al + sum(p[1:], p[0])
-        wb[rows, :] = wb[rows, :] * al + sum(w[1:], w[0])
-        p = jnp.concatenate([a.astype(BF16) for a in p], axis=1)
-        w = jnp.concatenate([a.astype(BF16) for a in w], axis=1)
-        pv = jnp.dot(p, kb[keys, 256:512], preferred_element_type=F32)
-        wv = jnp.dot(w, kb[keys, 256:384], preferred_element_type=F32)
-        acc[rows, :128] = acc[rows, :128] * al + pv[:, :128]
-        acc[rows, 128:256] = acc[rows, 128:256] * al + pv[:, 128:]
-        acc[rows, 256:384] = acc[rows, 256:384] * al + wv
+    def attend(first, keys, size):
+        cut = [slice(j * 128, (j + 1) * 128) for j in range(size // 128)]
+        halves = [pl.ds(pl.multiple_of(first + n * 256, 256), 256) for n in (0, 1)]
+
+        def scores(rows):
+            return (lax.dot_general(qb[rows, :128], kb[keys, 128:256], NT, preferred_element_type=F32),
+                    lax.dot_general(qb[rows, :], kb[keys, :256], NT, preferred_element_type=F32))
+
+        def soften(rows, s, t):
+            top = s[:, cut[0]]
+            for j in cut[1:]:
+                top = jnp.maximum(top, s[:, j])
+            top = jnp.broadcast_to(jnp.max(top, axis=1, keepdims=True), top.shape) * (SCALE * LOG2E)
+            old = mb[rows, :]
+            new = jnp.maximum(old, top)
+            p = [jnp.exp2(s[:, j] * (SCALE * LOG2E) - new) for j in cut]
+            w = [a * t[:, j] for a, j in zip(p, cut)]
+            return (new, jnp.exp2(old - new), sum(p[1:], p[0]), sum(w[1:], w[0]),
+                    jnp.concatenate([a.astype(BF16) for a in p], axis=1),
+                    jnp.concatenate([a.astype(BF16) for a in w], axis=1))
+
+        def products(p, w):
+            return (jnp.dot(p, kb[keys, 256:512], preferred_element_type=F32),
+                    jnp.dot(w, kb[keys, 256:384], preferred_element_type=F32))
+
+        s0 = scores(halves[0])
+        s1 = scores(halves[1])
+        e0 = soften(halves[0], *s0)
+        e1 = soften(halves[1], *s1)
+        o0 = products(*e0[4:])
+        o1 = products(*e1[4:])
+        for rows, (new, al, ps, ws, _, _), (pv, wv) in zip(halves, (e0, e1), (o0, o1)):
+            mb[rows, :] = new
+            lb[rows, :] = lb[rows, :] * al + ps
+            wb[rows, :] = wb[rows, :] * al + ws
+            acc[rows, :128] = acc[rows, :128] * al + pv[:, :128]
+            acc[rows, 128:256] = acc[rows, 128:256] * al + pv[:, 128:]
+            acc[rows, 256:384] = acc[rows, 256:384] * al + wv
 
     def small(b, carry):
         for i in range(6):
@@ -215,7 +229,7 @@
             def _():
                 small_events(i)
         g, k = pick(b, [e[0] for e in SMALL]), pick(b, [e[1] for e in SMALL])
-        attend(pl.ds(pl.multiple_of(g * 512, 512), 512), pl.ds(pl.multiple_of(k * 512, 512), 512), 4)
+        attend(g * 512, pl.ds(pl.multiple_of(k * 512, 512), 512), 512)
         return carry
 
     def large(b, carry):
@@ -224,7 +238,7 @@
             def _():
                 large_events(i)
         g, k = pick(b, [e[0] for e in LARGE]), pick(b, [e[1] for e in LARGE])
-        attend(pl.ds(pl.multiple_of(g * 512, 512), 512), pl.ds(pl.multiple_of(k * 1024, 1024), 1024), 8)
+        attend(g * 512, pl.ds(pl.multiple_of(k * 1024, 1024), 1024), 1024)
         for i in range(1, 5):
             @pl.when(b == i)
             def _():

time: 44.5 us -> 44.1 us (level)
  Pallas kernels: 42.9 us -> 42.3 us
    pallas_call x1, Pallas kernels: 42.9 us -> 42.3 us  [on_device(): pl.pallas_call(kernel, out_shape=jax.ShapeDtypeStruct((2 * TOK, HD), F32)...]
where the time goes in v5:
time: 44.1 us; the launch traced here: 43.6 us
  Pallas kernels  42.3 us (96%)
  local copies, waits for them, and re-layouts  0.66 us (1%)
  between operations  0.64 us (1%)
    pallas_call x1, Pallas kernels, on_device(): pl.pallas_call(kernel, out_shape=jax.ShapeDtypeStruct((2 * TOK, HD), F32)...  42.3 us

profile of v5, /device:TPU:1, one launch (start us, length us, event | category | flops | bytes accessed | tf_op | source)
XLA Modules:
  0.0 43.6 jit_solution(9627098984774627248)
XLA Ops:
  0.6 42.3 %shard_map.77 = f32[256,128]{1,0:T(8,128)S(1)} custom-call(bf16[128,128]{1,0:T(8,128)(2,1)} %q_ref.1, bf16[128,128]{1,0:T(8,128)(2,1)} %k_ref.1, bf16[128,128]{1,0:T(8,128)(2,1)} %v_ref.1, bf16[128,128]{1,0:T(8,128)(2,1)} %qt_ref.1, bf16[128,128]{1,0:T(8,128)(2,1)} %kt_ref.1, bf16[128,128]{1,0:T(8,128)(2,1)} %vt_ref.1), custom_call_target="tpu_custom_call" | custom-call | tf_op jit(solution)/shard_map/pallas_call | solution.py:329
  43.0 0.7 %fusion = (f32[128,128]{1,0:T(8,128)}, f32[128,128]{1,0:T(8,128)}) fusion(f32[256,128]{1,0:T(8,128)S(1)} %shard_map.77), kind=kLoop, calls=%fused_computation | loop fusion | bytes 262144 | tf_op jit(solution)/shard_map/slice | solution.py:357

commit v6 on v5

--- a/solution.py
+++ b/solution.py
@@ -56,7 +56,7 @@
                                                qb.at[pl.ds(h * 256, HALF), pl.ds(n * HD, HD)], in_s.at[4 + 2 * h + n]))
     for c in loads:
         c.start()
-    for c in loads:
+    for c in loads[:4]:
         c.wait()
     pl.semaphore_wait(barrier, 9)
 
@@ -101,6 +101,8 @@
         ring(1, h).start()
         ring(2, h).start()
         if h == 0:
+            for c in loads[4:]:
+                c.wait()
             for i in (1, 3, 2):
                 query1(0, i).start()
                 query1(1, i).start()

time: 44.1 us -> 44.1 us (level)
  no operation moved by 1% of the time
where the time goes in v6:
time: 44.1 us; the launch traced here: 43.6 us
  Pallas kernels  42.3 us (96%)
  local copies, waits for them, and re-layouts  0.66 us (1%)
  between operations  0.64 us (1%)
    pallas_call x1, Pallas kernels, on_device(): pl.pallas_call(kernel, out_shape=jax.ShapeDtypeStruct((2 * TOK, HD), F32)...  42.3 us

profile of v6, /device:TPU:1, one launch (start us, length us, event | category | flops | bytes accessed | tf_op | source)
XLA Modules:
  0.0 43.6 jit_solution(6778854460435871671)
XLA Ops:
  0.6 42.3 %shard_map.77 = f32[256,128]{1,0:T(8,128)S(1)} custom-call(bf16[128,128]{1,0:T(8,128)(2,1)} %q_ref.1, bf16[128,128]{1,0:T(8,128)(2,1)} %k_ref.1, bf16[128,128]{1,0:T(8,128)(2,1)} %v_ref.1, bf16[128,128]{1,0:T(8,128)(2,1)} %qt_ref.1, bf16[128,128]{1,0:T(8,128)(2,1)} %kt_ref.1, bf16[128,128]{1,0:T(8,128)(2,1)} %vt_ref.1), custom_call_target="tpu_custom_call" | custom-call | tf_op jit(solution)/shard_map/pallas_call | solution.py:331
  43.0 0.7 %fusion = (f32[128,128]{1,0:T(8,128)}, f32[128,128]{1,0:T(8,128)}) fusion(f32[256,128]{1,0:T(8,128)S(1)} %shard_map.77), kind=kLoop, calls=%fused_computation | loop fusion | bytes 262144 | tf_op jit(solution)/shard_map/slice | solution.py:359
